TPU v7x, 32 devices: a whole 2x2x4 slice. The times are simulated.
32 devices in a mesh: grp: 2 (over x), scan: 16 (over z, y, core).
Axes of the slice: x: 2, y: 2, z: 4, core: 2. Of those that a mesh axis runs over, the one named last changes fastest.
Arguments:
- patterns: bfloat16 [3072, 64, 256], P(('grp', 'scan')), parts along dimension 0, may hold values from -6 to 6
- templates: bfloat16 [32, 64, 256], P('scan'), may hold values from -6 to 6
- radius_bin: int32 [64], replicated, may hold values from 0 to 7
- radial_gain: float32 [8], replicated, may hold values from 0.25 to 4
- orientation: int32 [32, 1], replicated, may hold values from 0 to 15
Outputs:
- corr_map: float32 [3072, 32], P(('grp', 'scan')), parts along dimension 0
- orient_map: float32 [3072, 16], P(('grp', 'scan')), parts along dimension 0
There are 2 independent parts, one for each index of `grp`. A program takes and returns all parts, laid end to end along the dimension named above; an argument that names none is the same for every part. Nothing has to cross between parts.
Inputs may be any that keep to these rules, and one draw needn't show every extreme that they name: Every orientation group holds at least one template.
All inputs are finite; a program needn't handle non-finite values.
Results may differ from a plain program's by a relative error of at most 0.0024.
Values may be sent and summed in bfloat16 or wider, within the bound.
No kernel may reach another device: no remote copies, remote signals or barrier semaphores. Data moves between devices by JAX's collectives and lax.ppermute only.
A program may use at most 128 MiB of HBM per device.

v0:
```python
import math
import jax
import jax.numpy as jnp
from jax import lax
from jax.sharding import PartitionSpec as P

RADII = 64
ANGLES = 256
GAINS = 8
TMPL_PER_GROUP = 2


def with_halo(shard, sides, width):
    for axis, dim in sides:
        size, length = (lax.axis_size(axis), shard.shape[dim])
        up = [(i, (i + 1) % size) for i in range(size - 1)]
        down = [(j, i) for i, j in up]
        last = lax.slice_in_dim(shard, length - width, length, axis=dim)
        leading = lax.slice_in_dim(shard, 0, width, axis=dim)
        before = lax.ppermute(last, axis, up)
        after = lax.ppermute(leading, axis, down)
        shard = jnp.concatenate([before, shard, after], axis=dim)
    return shard


def make_tables():
    half = ANGLES // 2
    along = jnp.arange(ANGLES, dtype=jnp.int32)
    modes = jnp.arange(half + 1, dtype=jnp.int32)
    phase = 2.0 * math.pi / ANGLES * (along[:, None] * modes[None, :] % ANGLES).astype(jnp.float32)
    basis = jnp.concatenate([jnp.cos(phase), jnp.sin(phase[:, 1:half])], axis=1).astype(
        jnp.bfloat16
    )
    factor_norm = 1.0 / (ANGLES * math.sqrt(RADII * ANGLES))
    mode_weight = jnp.where((modes == 0) | (modes == half), 1.0, 2.0).astype(jnp.float32)
    phase_rows = phase.T
    inverse = jnp.concatenate(
        [mode_weight[:, None] * jnp.cos(phase_rows), -mode_weight[:, None] * jnp.sin(phase_rows)],
        axis=0,
    )
    return (basis, (inverse * factor_norm).astype(jnp.bfloat16))


def spectrum(raw, basis):
    count = raw.shape[0]
    flat = raw.reshape(-1, ANGLES)
    spec = lax.dot_general(
        basis, flat, (((0,), (1,)), ((), ())), preferred_element_type=jnp.float32
    )
    return spec.reshape(ANGLES, count, RADII)


def mode_products(left, right):
    return jnp.einsum("kpr,ktr->ktp", left, right, preferred_element_type=jnp.float32)


def correlate(pat_spec, tmpl_spec, inverse):
    half = ANGLES // 2
    count = tmpl_spec.shape[1]
    pos_count = pat_spec.shape[1]
    pat_cos = pat_spec[: half + 1]
    pat_sin = pat_spec[half + 1 :]
    tmpl_cos = tmpl_spec[: half + 1]
    tmpl_sin = tmpl_spec[half + 1 :]
    both_cos = mode_products(pat_cos, tmpl_cos)
    both_sin = mode_products(pat_sin, tmpl_sin)
    cos_sin = mode_products(pat_cos[1:half], tmpl_sin)
    sin_cos = mode_products(pat_sin, tmpl_cos[1:half])
    edge = jnp.zeros((1, count, pos_count), jnp.float32)
    real_part = both_cos + jnp.concatenate([edge, both_sin, edge], axis=0)
    imag_part = jnp.concatenate([edge, cos_sin - sin_cos, edge], axis=0)
    cross = jnp.concatenate([real_part, imag_part], axis=0).astype(jnp.bfloat16)
    cross = cross.reshape(2 * (half + 1), count * pos_count)
    shifted = lax.dot_general(
        inverse, cross, (((0,), (0,)), ((), ())), preferred_element_type=jnp.float32
    )
    return jnp.max(shifted, axis=0).reshape(count, pos_count)


def block_of(count, limit):
    size = limit
    while size > 1:
        if count % size == 0:
            return size
        size = size // 2
    return 1


def correlate_into(carry, pat_spec, count, prepare, inverse):
    block_size = block_of(count, 64)

    def step(index, total):
        begin = index * block_size
        values = correlate(pat_spec, prepare(begin, block_size), inverse)
        return lax.dynamic_update_slice(total, values, (begin, jnp.int32(0)))

    return lax.fori_loop(0, count // block_size, step, carry)


def on_device(patterns, templates, radius_bin, radial_gain, orientation):
    basis, inverse = make_tables()
    pos_count = patterns.shape[0]
    total_tmpl = templates.shape[0] * lax.axis_size("scan")
    group_count = total_tmpl // TMPL_PER_GROUP
    onehot = (radius_bin[:, None] == jnp.arange(GAINS, dtype=jnp.int32)[None, :]).astype(
        jnp.float32
    )
    radius_weight = jnp.sum(onehot * radial_gain[None, :], axis=1)
    pat_spec = (spectrum(patterns, basis) * radius_weight[None, None, :]).astype(jnp.bfloat16)
    initial = jnp.zeros((total_tmpl, pos_count), jnp.float32)

    def raw_rows(piece):
        return lambda begin, size: spectrum(
            lax.dynamic_slice_in_dim(piece, begin, size, 0), basis
        ).astype(jnp.bfloat16)

    piece = lax.all_gather(templates, "scan", axis=0, tiled=True)
    by_template = correlate_into(initial, pat_spec, piece.shape[0], raw_rows(piece), inverse)
    corr_map = by_template.T
    groups = orientation[:, 0]
    member = groups[None, :] == jnp.arange(group_count, dtype=jnp.int32)[:, None]
    group_block = block_of(group_count, 16)
    member_blocks = member.reshape(group_count // group_block, group_block, total_tmpl)

    def group_max(mask):
        return jnp.max(jnp.where(mask[:, :, None], by_template[None, :, :], -jnp.inf), axis=1)

    best = lax.map(group_max, member_blocks).reshape(group_count, pos_count).T
    padded = with_halo(best, (("scan", 0),), 1)
    orient_map = 0.25 * (padded[:-2] + 2.0 * best + padded[2:])
    return (corr_map, orient_map)


def solution(mesh):
    placed = (P(("grp", "scan"), None, None), P("scan", None, None), P(), P(), P())
    return jax.shard_map(
        on_device,
        mesh=mesh,
        in_specs=placed,
        out_specs=(P(("grp", "scan"), None), P(("grp", "scan"), None)),
        check_vma=False,
    )
```

profile of v0, /device:TPU:5, one launch (start us, length us, event | category | flops | bytes accessed | tf_op | source)
XLA Modules:
  0.0 101.3 jit_solution(18244889343172042133)
XLA Ops:
  7.2 0.0 copy-start
  7.2 0.0 all-gather.2.cloned.1.call-start
  7.2 0.7 all-gather.2.cloned.1.call-update
  7.9 1.0 select_reduce_fusion.1
  8.9 1.0 cosine_convert_fusion
  9.8 0.1 fusion.19
  10.0 0.5 fusion.31
  10.5 0.0 copy-done
  10.5 3.6 %multiply_convert_fusion = bf16[256,96,64]{0,1,2:T(8,128)(2,1)S(1)} fusion(f32[64]{0:T(128)S(1)} %select_reduce_fusion.1, bf16[96,64,256]{2,1,0:T(8,128)(2,1)S(1)} %copy-done, bf16[256,127]{1,0:T(8,128)(2,1)S(1)} %fusion.31, bf16[256,129]{1,0:T(8,128)(2,1)S(1)} %cosine_convert_fusion), kind=kOutput, calls=%fused_computation | convolution fusion | flops 808714240 | bytes 6422784 | tf_op jit(solution)/shard_map/dot_general | solution.py:47
  14.1 0.0 copy-start.2
  14.1 2.7 %fusion.41 = (bf16[127,96,64]{0,1,2:T(8,128)(2,1)}, bf16[127,96,64]{0,1,2:T(8,128)(2,1)}) fusion(bf16[256,96,64]{0,1,2:T(8,128)(2,1)S(1)} %multiply_convert_fusion), kind=kLoop, calls=%fused_computation.59 | loop fusion | bytes 6242304 | tf_op jit(solution)/shard_map/while/body/eval_jaxpr/slice | solution.py:62
  16.9 0.0 copy-done.2
  16.9 4.0 %copy.44 = bf16[127,96,64]{1,2,0:T(8,128)(2,1)} copy(bf16[127,96,64]{0,1,2:T(8,128)(2,1)} %get-tuple-element.28) | data formatting | bytes 3121152 | tf_op jit(solution)/shard_map/while/body/eval_jaxpr/slice | solution.py:67
  20.9 4.0 %copy.42 = bf16[127,96,64]{1,2,0:T(8,128)(2,1)} copy(bf16[127,96,64]{0,1,2:T(8,128)(2,1)} %get-tuple-element.20) | data formatting | bytes 3121152 | tf_op jit(solution)/shard_map/while/body/eval_jaxpr/slice | solution.py:62
  24.9 0.0 copy-start.8
  24.9 5.0 %copy.40 = bf16[129,96,64]{1,2,0:T(8,128)(2,1)} copy(bf16[129,96,64]{0,1,2:T(8,128)(2,1)} %bitcast.19) | data formatting | bytes 3170304 | tf_op jit(solution)/shard_map/while/body/eval_jaxpr/slice | solution.py:61
  29.8 0.0 copy-done.8
  29.9 1.2 %sine_multiply_fusion = (f32[129,256]{1,0:T(8,128)S(1)}, f32[129,256]{1,0:T(8,128)}) fusion(f32[129]{0:T(256)S(1)} %fusion.35, f32[129]{0:T(256)S(1)} %or_select_fusion), kind=kLoop, calls=%fused_computation.35 | loop fusion | flops 528384 | bytes 265224 | tf_op jit(solution)/shard_map/mul | solution.py:38
  31.1 17.7 %all-gather.2.cloned.1.call-done = bf16[32,64,256]{2,1,0:T(8,128)(2,1)} async-done(((bf16[2,64,256]{2,1,0:T(8,128)(2,1)}), bf16[32,64,256]{2,1,0:T(8,128)(2,1)}) %all-gather.2.cloned.1.call-update) | async-done | bytes 1048592 | tf_op jit(solution)/shard_map/all_gather | solution.py:117
  48.8 1.7 %convolution_convert_fusion = bf16[256,32,64]{0,2,1:T(8,128)(2,1)S(1)} fusion(bf16[32,64,256]{2,1,0:T(8,128)(2,1)} %all-gather.2.cloned.1.call-done, bf16[256,127]{1,0:T(8,128)(2,1)S(1)} %fusion.31, bf16[256,129]{1,0:T(8,128)(2,1)S(1)} %cosine_convert_fusion), kind=kOutput, calls=%fused_computation.14 | convolution fusion | flops 269221888 | bytes 2228224 | tf_op jit(solution)/shard_map/while/body/eval_jaxpr/dot_general | solution.py:47
  50.6 0.0 copy-start.3
  50.6 0.9 copy-done.3
  51.5 1.4 %fusion.42 = (bf16[127,32,64]{0,2,1:T(8,128)(2,1)}, bf16[127,32,64]{0,2,1:T(8,128)(2,1)}) fusion(bf16[256,32,64]{0,2,1:T(8,128)(2,1)S(1)} %convolution_convert_fusion), kind=kLoop, calls=%fused_computation.60 | loop fusion | bytes 2080768 | tf_op jit(solution)/shard_map/while/body/eval_jaxpr/slice | solution.py:68
  52.9 3.5 %copy.41 = bf16[127,32,64]{2,1,0:T(8,128)(2,1)} copy(bf16[127,32,64]{0,2,1:T(8,128)(2,1)} %get-tuple-element.30) | data formatting | bytes 1040384 | tf_op jit(solution)/shard_map/while/body/eval_jaxpr/slice | solution.py:64
  56.4 3.5 %copy.45 = bf16[127,32,64]{2,1,0:T(8,128)(2,1)} copy(bf16[127,32,64]{0,2,1:T(8,128)(2,1)} %get-tuple-element.29) | data formatting | bytes 1040384 | tf_op jit(solution)/shard_map/while/body/eval_jaxpr/slice | solution.py:68
  59.9 0.0 copy-start.1
  59.9 2.7 %fusion.45 = f32[127,32,96]{2,1,0:T(8,128)S(1)} fusion(bf16[127,32,64]{2,1,0:T(8,128)(2,1)} %copy.41, bf16[127,96,64]{1,2,0:T(8,128)(2,1)} %copy.44), kind=kOutput, calls=%fused_computation.63 | convolution fusion | flops 49938432 | bytes 3641344 | tf_op jit(solution)/shard_map/while/body/eval_jaxpr/kpr,ktr->ktp/dot_general | solution.py:54
  62.6 0.0 copy-done.1
  62.6 0.1 copy-done.4
  62.7 2.0 %fusion.44 = f32[127,32,96]{2,1,0:T(8,128)} fusion(bf16[127,32,64]{2,1,0:T(8,128)(2,1)S(1)} %copy-done.4, bf16[127,96,64]{1,2,0:T(8,128)(2,1)S(1)} %copy-done.1), kind=kOutput, calls=%fused_computation.62 | convolution fusion | flops 49938432 | bytes 3641344 | tf_op jit(solution)/shard_map/while/body/eval_jaxpr/kpr,ktr->ktp/dot_general | solution.py:54
  64.7 0.0 copy-done.5
  64.7 1.7 %subtract_convert_fusion = bf16[127,32,96]{2,1,0:T(8,128)(2,1)} fusion(f32[127,32,96]{2,1,0:T(8,128)S(1)} %fusion.45, bf16[127,32,64]{2,1,0:T(8,128)(2,1)S(1)} %copy-done.5, bf16[127,96,64]{1,2,0:T(8,128)(2,1)S(1)} %copy-done.1), kind=kOutput, calls=%fused_computation.5 | convolution fusion | flops 50718720 | bytes 4421632 | tf_op jit(solution)/shard_map/while/body/eval_jaxpr/kpr,ktr->ktp/dot_general | solution.py:54
  66.4 2.7 %copy.47 = bf16[127,32,96]{0,2,1:T(8,128)(2,1)} copy(bf16[127,32,96]{2,1,0:T(8,128)(2,1)} %subtract_convert_fusion) | data formatting | bytes 1560576 | tf_op jit(solution)/shard_map/convert.4
  69.1 2.4 %copy.48 = bf16[127,3072]{1,0:T(8,128)(2,1)} copy(bf16[127,3072]{0,1:T(8,128)(2,1)} %bitcast.21) | data formatting | bytes 1560576 | tf_op jit(solution)/shard_map/while/body/eval_jaxpr/concatenate | solution.py:72
  71.5 2.8 %copy.39 = bf16[129,32,64]{2,1,0:T(8,128)(2,1)} copy(bf16[129,32,64]{0,2,1:T(8,128)(2,1)} %bitcast.20) | data formatting | bytes 1056768 | tf_op jit(solution)/shard_map/while/body/eval_jaxpr/slice | solution.py:63
  74.3 4.3 %fusion.4 = bf16[129,32,96]{2,1,0:T(8,128)(2,1)} fusion(f32[1,32,96]{2,1,0:T(8,128)S(1)} %broadcast.63, f32[127,32,96]{2,1,0:T(8,128)} %fusion.44, bf16[129,32,64]{2,1,0:T(8,128)(2,1)} %copy.39, bf16[129,96,64]{1,2,0:T(8,128)(2,1)} %copy.40), kind=kOutput, calls=%fused_computation.4 | convolution fusion | flops 52310016 | bytes 4478976 | tf_op jit(solution)/shard_map/while/body/eval_jaxpr/kpr,ktr->ktp/dot_general | solution.py:54
  78.6 3.4 %concatenate.33 = bf16[129,3072]{1,0:T(8,128)(2,1)} reshape(bf16[129,32,96]{2,1,0:T(8,128)(2,1)} %fusion.4) | data formatting | bytes 1585152 | tf_op jit(solution)/shard_map/while/body/eval_jaxpr/concatenate | solution.py:72
  81.9 0.0 copy-done.6
  82.0 2.5 %fusion.13 = f32[3072]{0:T(1024)S(1)} fusion(bf16[1,3072]{1,0:T(2,128)(2,1)S(1)} %concatenate.34, bf16[127,3072]{1,0:T(8,128)(2,1)} %copy.48, bf16[129,3072]{1,0:T(8,128)(2,1)} %concatenate.33, f32[129,256]{1,0:T(8,128)S(1)} %get-tuple-element.37, f32[129,256]{1,0:T(8,128)S(1)} %copy-done.6), kind=kOutput, calls=%fused_computation.15 | convolution fusion | flops 413121024 | bytes 1855488 | tf_op jit(solution)/shard_map/while/body/eval_jaxpr/dot_general | solution.py:74
  84.4 0.1 reshape.51
  84.5 0.1 select_reduce_fusion
  84.6 0.1 fusion.43
  84.7 3.2 %collective-permute-start = (f32[1,16]{0,1:T(8,128)S(1)}, f32[1,16]{0,1:T(8,128)S(1)}, u32[]{:S(2)}, u32[]{:S(2)}) collective-permute-start(f32[1,16]{0,1:T(8,128)S(1)} %get-tuple-element.31), channel_id=1, source_target_pairs={{0,1},{1,2},{2,3},{3,4},{4,5},{5,6},{6,7},{7,8},{8,9},{9,10},{10,1... | collective-permute-start | bytes 200 | tf_op jit(solution)/shard_map/ppermute | solution.py:20
  87.9 1.9 %collective-permute-start.1 = (f32[1,16]{0,1:T(8,128)S(1)}, f32[1,16]{0,1:T(8,128)S(1)}, u32[]{:S(2)}, u32[]{:S(2)}) collective-permute-start(f32[1,16]{0,1:T(8,128)S(1)} %get-tuple-element.36), channel_id=1, source_target_pairs={{1,0},{2,1},{3,2},{4,3},{5,4},{6,5},{7,6},{8,7},{9,8},{10,9},{11,1... | collective-permute-start | bytes 200 | tf_op jit(solution)/shard_map/ppermute | solution.py:21
  89.9 0.0 collective-permute-done
  89.9 3.9 %collective-permute-done.1 = f32[1,16]{0,1:T(8,128)S(1)} collective-permute-done((f32[1,16]{0,1:T(8,128)S(1)}, f32[1,16]{0,1:T(8,128)S(1)}, u32[]{:S(2)}, u32[]{:S(2)}) %collective-permute-start.1) | collective-permute-done | bytes 96 | tf_op jit(solution)/shard_map/ppermute | solution.py:21
  93.8 0.7 fusion.33
  94.5 0.0 copy-done.7
  (9 shorter events, 0.0 us)
Async XLA Ops:
  7.2 3.3 %copy-start = (bf16[96,64,256]{2,1,0:T(8,128)(2,1)S(1)}, bf16[96,64,256]{2,1,0:T(8,128)(2,1)}, u32[]{:S(2)}) copy-start(bf16[96,64,256]{2,1,0:T(8,128)(2,1)} %param.5) | copy-start | bytes 9437188
  7.2 41.6 %all-gather.2.cloned.1.call-start = ((), (), s32[]{:S(2)}) async-start(), calls=%async_computation | async-start | bytes 1114112 | tf_op jit(solution)/shard_map/all_gather | solution.py:117
  14.1 2.7 %copy-start.2 = (bf16[256,96,64]{0,1,2:T(8,128)(2,1)}, bf16[256,96,64]{0,1,2:T(8,128)(2,1)S(1)}, u32[]{:S(2)}) copy-start(bf16[256,96,64]{0,1,2:T(8,128)(2,1)S(1)} %multiply_convert_fusion) | copy-start | bytes 9437188
  24.9 5.0 %copy-start.8 = (s32[32,1]{0,1:T(1,128)S(1)}, s32[32,1]{0,1:T(1,128)}, u32[]{:S(2)}) copy-start(s32[32,1]{0,1:T(1,128)} %param.9) | copy-start | bytes 388
  50.6 1.0 copy-start.3
  59.9 2.7 %copy-start.1 = (bf16[127,96,64]{1,2,0:T(8,128)(2,1)S(1)}, bf16[127,96,64]{1,2,0:T(8,128)(2,1)}, u32[]{:S(2)}) copy-start(bf16[127,96,64]{1,2,0:T(8,128)(2,1)} %copy.42) | copy-start | bytes 4681732
  59.9 2.8 %copy-start.4 = (bf16[127,32,64]{2,1,0:T(8,128)(2,1)S(1)}, bf16[127,32,64]{2,1,0:T(8,128)(2,1)}, u32[]{:S(2)}) copy-start(bf16[127,32,64]{2,1,0:T(8,128)(2,1)} %copy.41) | copy-start | bytes 1560580
  62.7 2.0 %copy-start.5 = (bf16[127,32,64]{2,1,0:T(8,128)(2,1)S(1)}, bf16[127,32,64]{2,1,0:T(8,128)(2,1)}, u32[]{:S(2)}) copy-start(bf16[127,32,64]{2,1,0:T(8,128)(2,1)} %copy.45) | copy-start | bytes 1560580
  74.3 7.6 %copy-start.6 = (f32[129,256]{1,0:T(8,128)S(1)}, f32[129,256]{1,0:T(8,128)}, u32[]{:S(2)}) copy-start(f32[129,256]{1,0:T(8,128)} %get-tuple-element.38) | copy-start | bytes 396292
  84.5 10.0 %copy-start.7 = (f32[32,96]{1,0:T(8,128)}, f32[32,96]{1,0:T(8,128)S(1)}, u32[]{:S(2)}) copy-start(f32[32,96]{1,0:T(8,128)S(1)} %reshape.51) | copy-start | bytes 36868
  84.7 5.2 %collective-permute-start = (f32[1,16]{0,1:T(8,128)S(1)}, f32[1,16]{0,1:T(8,128)S(1)}, u32[]{:S(2)}, u32[]{:S(2)}) collective-permute-start(f32[1,16]{0,1:T(8,128)S(1)} %get-tuple-element.31), channel_id=1, source_target_pairs={{0,1},{1,2},{2,3},{3,4},{4,5},{5,6},{6,7},{7,8},{8,9},{9,10},{10,1... | collective-permute-start | bytes 200 | tf_op jit(solution)/shard_map/ppermute | solution.py:20
  87.9 5.9 %collective-permute-start.1 = (f32[1,16]{0,1:T(8,128)S(1)}, f32[1,16]{0,1:T(8,128)S(1)}, u32[]{:S(2)}, u32[]{:S(2)}) collective-permute-start(f32[1,16]{0,1:T(8,128)S(1)} %get-tuple-element.36), channel_id=1, source_target_pairs={{1,0},{2,1},{3,2},{4,3},{5,4},{6,5},{7,6},{8,7},{9,8},{10,9},{11,1... | collective-permute-start | bytes 200 | tf_op jit(solution)/shard_map/ppermute | solution.py:21
Sparse Core Ops, SparseCore 0:
  10.2 38.5 all-gather.1
where the time goes:
time: 102 us; the launch traced here: 101 us
  local copies, waits for them, and re-layouts  36.6 us (36%)
  waiting for transfers between devices  22.3 us (22%)
  matrix products  18.5 us (18%)
  between operations  14.2 us (14%)
  starting transfers between devices  5.19 us (5%)
  other arithmetic  4.61 us (5%)
    all_gather x1, waiting for transfers between devices, on_device(): piece = lax.all_gather(templates, 'scan', axis=0, tiled=True)  17.7 us
    dot_general x4, matrix products, mode_products(): jnp.einsum('kpr,ktr->ktp', left, right, preferred_element_type=jnp.float32)  10.6 us
    slice x2, local copies, waits for them, and re-layouts, correlate(): pat_sin = pat_spec[half + 1:]  6.72 us
    concatenate x3, local copies, waits for them, and re-layouts, correlate(): cross = jnp.concatenate([real_part, imag_part], axis=0).astype(jnp.bfloat16)  5.75 us
    dot_general x2, matrix products, spectrum(): lax.dot_general(basis, flat, (((0,), (1,)), ((), ())), preferred_element_...  5.37 us
    slice x1, local copies, waits for them, and re-layouts, correlate(): pat_cos = pat_spec[:half + 1]  4.96 us
    slice x2, local copies, waits for them, and re-layouts, correlate(): sin_cos = mode_products(pat_sin, tmpl_cos[1:half])  4.9 us
    slice x1, local copies, waits for them, and re-layouts, correlate(): cos_sin = mode_products(pat_cos[1:half], tmpl_sin)  4 us
  transfers between devices with their start and end apart: 3, of which 2 were waited for; matrix products, arithmetic and copies ran while one was open for 23% of the time, Pallas kernels for 0%

commit v1 on v0

--- a/solution.py
+++ b/solution.py
@@ -8,6 +8,27 @@
 ANGLES = 256
 GAINS = 8
 TMPL_PER_GROUP = 2
+
+
+def gather_around(x, axis, dim):
+    size, index, rows = (lax.axis_size(axis), lax.axis_index(axis), x.shape[dim])
+    forward = [(i, (i + 1) % size) for i in range(size)]
+    downward = [(i, (i - 1) % size) for i in range(size)]
+    filled = jnp.zeros((*x.shape[:dim], size * rows, *x.shape[dim + 1 :]), x.dtype)
+    filled = lax.dynamic_update_slice_in_dim(filled, x, index * rows, axis=dim)
+    from_left = from_right = x
+    half = size // 2
+    for turn in range(1, half + 1):
+        from_left = lax.ppermute(from_left, axis, forward)
+        filled = lax.dynamic_update_slice_in_dim(
+            filled, from_left, (index - turn) % size * rows, axis=dim
+        )
+        if turn < size - half:
+            from_right = lax.ppermute(from_right, axis, downward)
+            filled = lax.dynamic_update_slice_in_dim(
+                filled, from_right, (index + turn) % size * rows, axis=dim
+            )
+    return filled
 
 
 def with_halo(shard, sides, width):
@@ -114,7 +135,7 @@
             lax.dynamic_slice_in_dim(piece, begin, size, 0), basis
         ).astype(jnp.bfloat16)
 
-    piece = lax.all_gather(templates, "scan", axis=0, tiled=True)
+    piece = gather_around(templates, "scan", 0)
     by_template = correlate_into(initial, pat_spec, piece.shape[0], raw_rows(piece), inverse)
     corr_map = by_template.T
     groups = orientation[:, 0]

time: 102 us -> 117 us (1.15)
  the two profiles are of different devices: /device:TPU:5 before, /device:TPU:0 now
where the time goes in v1:
time: 117 us; the launch traced here: 116 us
  local copies, waits for them, and re-layouts  38.5 us (33%)
  starting transfers between devices  36.7 us (31%)
  matrix products  17.2 us (15%)
  waiting for transfers between devices  17.1 us (15%)
  other arithmetic  5.58 us (5%)
    ppermute x7, starting transfers between devices, gather_around(): from_right = lax.ppermute(from_right, axis, downward)  31.8 us
    ppermute x8, waiting for transfers between devices, gather_around(): from_left = lax.ppermute(from_left, axis, forward)  16.1 us
    dot_general x4, matrix products, mode_products(): jnp.einsum('kpr,ktr->ktp', left, right, preferred_element_type=jnp.float32)  10.6 us
    slice x2, local copies, waits for them, and re-layouts, correlate(): pat_sin = pat_spec[half + 1:]  6.71 us
    concatenate x3, local copies, waits for them, and re-layouts, correlate(): cross = jnp.concatenate([real_part, imag_part], axis=0).astype(jnp.bfloat16)  5.73 us
    slice x1, local copies, waits for them, and re-layouts, correlate(): pat_cos = pat_spec[:half + 1]  4.99 us
    slice x2, local copies, waits for them, and re-layouts, correlate(): sin_cos = mode_products(pat_sin, tmpl_cos[1:half])  4.86 us
    dot_general x2, matrix products, spectrum(): lax.dot_general(basis, flat, (((0,), (1,)), ((), ())), preferred_element_...  4.14 us
  transfers between devices with their start and end apart: 17, of which 8 were waited for; matrix products, arithmetic and copies ran while one was open for 22% of the time, Pallas kernels for 0%

profile of v1, /device:TPU:0, one launch (start us, length us, event | category | flops | bytes accessed | tf_op | source)
XLA Modules:
  0.0 116.0 jit_solution(3415660139846758389)
XLA Ops:
  0.6 0.5 collective-permute-start
  1.1 5.1 %collective-permute-start.1 = (bf16[2,64,256]{2,1,0:T(8,128)(2,1)}, bf16[2,64,256]{2,1,0:T(8,128)(2,1)}, u32[]{:S(2)}, u32[]{:S(2)}) collective-permute-start(bf16[2,64,256]{2,1,0:T(8,128)(2,1)} %param.6), channel_id=1, source_target_pairs={{0,15},{1,0},{2,1},{3,2},{4,3},{5,4},{6,5},{7,6},{8,7},{9,8},{10,9... | collective-permute-start | bytes 196616 | tf_op jit(solution)/shard_map/ppermute | solution.py:27
  6.2 0.1 fusion.19
  6.3 1.0 cosine_convert_fusion
  7.3 0.5 fusion.31
  7.8 0.8 select_reduce_fusion.1
  8.6 3.6 %multiply_convert_fusion = bf16[256,96,64]{0,1,2:T(8,128)(2,1)S(1)} fusion(f32[64]{0:T(128)S(1)} %select_reduce_fusion.1, bf16[96,64,256]{2,1,0:T(8,128)(2,1)S(1)} %copy-done, bf16[256,127]{1,0:T(8,128)(2,1)S(1)} %fusion.31, bf16[256,129]{1,0:T(8,128)(2,1)S(1)} %cosine_convert_fusion), kind=kOutput, calls=%fused_computation | convolution fusion | flops 808714240 | bytes 6422784 | tf_op jit(solution)/shard_map/dot_general | solution.py:68
  12.2 2.7 %fusion.41 = (bf16[127,96,64]{0,1,2:T(8,128)(2,1)}, bf16[127,96,64]{0,1,2:T(8,128)(2,1)}) fusion(bf16[256,96,64]{0,1,2:T(8,128)(2,1)S(1)} %multiply_convert_fusion), kind=kLoop, calls=%fused_computation.75 | loop fusion | bytes 6242304 | tf_op jit(solution)/shard_map/while/body/eval_jaxpr/slice | solution.py:83
  15.0 4.0 %copy.33 = bf16[127,96,64]{1,2,0:T(8,128)(2,1)} copy(bf16[127,96,64]{0,1,2:T(8,128)(2,1)} %get-tuple-element.28) | data formatting | bytes 3121152 | tf_op jit(solution)/shard_map/while/body/eval_jaxpr/slice | solution.py:88
  19.0 4.0 %copy.31 = bf16[127,96,64]{1,2,0:T(8,128)(2,1)} copy(bf16[127,96,64]{0,1,2:T(8,128)(2,1)} %get-tuple-element.20) | data formatting | bytes 3121152 | tf_op jit(solution)/shard_map/while/body/eval_jaxpr/slice | solution.py:83
  23.0 5.0 %copy.29 = bf16[129,96,64]{1,2,0:T(8,128)(2,1)} copy(bf16[129,96,64]{0,1,2:T(8,128)(2,1)} %bitcast.19) | data formatting | bytes 3170304 | tf_op jit(solution)/shard_map/while/body/eval_jaxpr/slice | solution.py:82
  28.0 0.5 sine_multiply_fusion
  28.5 1.2 %cosine_multiply_fusion = f32[129,256]{1,0:T(8,128)} fusion(f32[129]{0:T(256)S(1)} %get-tuple-element.37), kind=kLoop, calls=%fused_computation.36 | loop fusion | flops 495360 | bytes 132612 | tf_op jit(solution)/shard_map/mul | solution.py:59
  29.7 0.7 iota_compare_fusion
  30.6 4.4 %collective-permute-start.3 = (bf16[2,64,256]{2,1,0:T(8,128)(2,1)}, bf16[2,64,256]{2,1,0:T(8,128)(2,1)S(1)}, u32[]{:S(2)}, u32[]{:S(2)}) collective-permute-start(bf16[2,64,256]{2,1,0:T(8,128)(2,1)} %collective-permute-done.1), channel_id=1, source_target_pairs={{0,15},{1,0},{2,1},{3,2},{4,3},{5,4},{6,5},{7,6},{8,7},{9,8},{10,9... | collective-permute-start | bytes 196616 | tf_op jit(solution)/shard_map/ppermute | solution.py:27
  35.0 0.8 constant_dynamic-update-slice_fusion.14
  35.8 0.8 constant_dynamic-update-slice_fusion.13
  36.7 0.5 collective-permute-done.2
  37.2 4.4 %collective-permute-start.5 = (bf16[2,64,256]{2,1,0:T(8,128)(2,1)S(1)}, bf16[2,64,256]{2,1,0:T(8,128)(2,1)S(1)}, u32[]{:S(2)}, u32[]{:S(2)}) collective-permute-start(bf16[2,64,256]{2,1,0:T(8,128)(2,1)S(1)} %collective-permute-done.3), channel_id=1, source_target_pairs={{0,15},{1,0},{2,1},{3,2},{4,3},{5,4},{6,5},{7,6},{8,7},{9,8},{10,9... | collective-permute-start | bytes 196616 | tf_op jit(solution)/shard_map/ppermute | solution.py:27
  41.7 1.9 %collective-permute-done.4 = bf16[2,64,256]{2,1,0:T(8,128)(2,1)S(1)} collective-permute-done((bf16[2,64,256]{2,1,0:T(8,128)(2,1)S(1)}, bf16[2,64,256]{2,1,0:T(8,128)(2,1)S(1)}, u32[]{:S(2)}, u32[]{:S(2)}) %collective-permute-start.4) | collective-permute-done | bytes 65568 | tf_op jit(solution)/shard_map/ppermute | solution.py:22
  43.6 4.5 %collective-permute-start.7 = (bf16[2,64,256]{2,1,0:T(8,128)(2,1)S(1)}, bf16[2,64,256]{2,1,0:T(8,128)(2,1)S(1)}, u32[]{:S(2)}, u32[]{:S(2)}) collective-permute-start(bf16[2,64,256]{2,1,0:T(8,128)(2,1)S(1)} %collective-permute-done.5), channel_id=1, source_target_pairs={{0,15},{1,0},{2,1},{3,2},{4,3},{5,4},{6,5},{7,6},{8,7},{9,8},{10,9... | collective-permute-start | bytes 196616 | tf_op jit(solution)/shard_map/ppermute | solution.py:27
  48.1 1.9 %collective-permute-done.6 = bf16[2,64,256]{2,1,0:T(8,128)(2,1)S(1)} collective-permute-done((bf16[2,64,256]{2,1,0:T(8,128)(2,1)S(1)}, bf16[2,64,256]{2,1,0:T(8,128)(2,1)S(1)}, u32[]{:S(2)}, u32[]{:S(2)}) %collective-permute-start.6) | collective-permute-done | bytes 65568 | tf_op jit(solution)/shard_map/ppermute | solution.py:22
  50.0 4.5 %collective-permute-start.9 = (bf16[2,64,256]{2,1,0:T(8,128)(2,1)S(1)}, bf16[2,64,256]{2,1,0:T(8,128)(2,1)S(1)}, u32[]{:S(2)}, u32[]{:S(2)}) collective-permute-start(bf16[2,64,256]{2,1,0:T(8,128)(2,1)S(1)} %collective-permute-done.7), channel_id=1, source_target_pairs={{0,15},{1,0},{2,1},{3,2},{4,3},{5,4},{6,5},{7,6},{8,7},{9,8},{10,9... | collective-permute-start | bytes 196616 | tf_op jit(solution)/shard_map/ppermute | solution.py:27
  54.5 1.9 %collective-permute-done.8 = bf16[2,64,256]{2,1,0:T(8,128)(2,1)S(1)} collective-permute-done((bf16[2,64,256]{2,1,0:T(8,128)(2,1)S(1)}, bf16[2,64,256]{2,1,0:T(8,128)(2,1)S(1)}, u32[]{:S(2)}, u32[]{:S(2)}) %collective-permute-start.8) | collective-permute-done | bytes 65568 | tf_op jit(solution)/shard_map/ppermute | solution.py:22
  56.4 4.5 %collective-permute-start.11 = (bf16[2,64,256]{2,1,0:T(8,128)(2,1)S(1)}, bf16[2,64,256]{2,1,0:T(8,128)(2,1)S(1)}, u32[]{:S(2)}, u32[]{:S(2)}) collective-permute-start(bf16[2,64,256]{2,1,0:T(8,128)(2,1)S(1)} %collective-permute-done.9), channel_id=1, source_target_pairs={{0,15},{1,0},{2,1},{3,2},{4,3},{5,4},{6,5},{7,6},{8,7},{9,8},{10,9... | collective-permute-start | bytes 196616 | tf_op jit(solution)/shard_map/ppermute | solution.py:27
  60.9 1.9 %collective-permute-done.10 = bf16[2,64,256]{2,1,0:T(8,128)(2,1)S(1)} collective-permute-done((bf16[2,64,256]{2,1,0:T(8,128)(2,1)S(1)}, bf16[2,64,256]{2,1,0:T(8,128)(2,1)S(1)}, u32[]{:S(2)}, u32[]{:S(2)}) %collective-permute-start.10) | collective-permute-done | bytes 65568 | tf_op jit(solution)/shard_map/ppermute | solution.py:22
  62.8 4.5 %collective-permute-start.13 = (bf16[2,64,256]{2,1,0:T(8,128)(2,1)S(1)}, bf16[2,64,256]{2,1,0:T(8,128)(2,1)S(1)}, u32[]{:S(2)}, u32[]{:S(2)}) collective-permute-start(bf16[2,64,256]{2,1,0:T(8,128)(2,1)S(1)} %collective-permute-done.11), channel_id=1, source_target_pairs={{0,15},{1,0},{2,1},{3,2},{4,3},{5,4},{6,5},{7,6},{8,7},{9,8},{10,9... | collective-permute-start | bytes 196616 | tf_op jit(solution)/shard_map/ppermute | solution.py:27
  67.3 1.9 %collective-permute-done.12 = bf16[2,64,256]{2,1,0:T(8,128)(2,1)S(1)} collective-permute-done((bf16[2,64,256]{2,1,0:T(8,128)(2,1)S(1)}, bf16[2,64,256]{2,1,0:T(8,128)(2,1)S(1)}, u32[]{:S(2)}, u32[]{:S(2)}) %collective-permute-start.12) | collective-permute-done | bytes 65568 | tf_op jit(solution)/shard_map/ppermute | solution.py:22
  69.2 6.3 %collective-permute-done.14 = bf16[2,64,256]{2,1,0:T(8,128)(2,1)S(1)} collective-permute-done((bf16[2,64,256]{2,1,0:T(8,128)(2,1)S(1)}, bf16[2,64,256]{2,1,0:T(8,128)(2,1)S(1)}, u32[]{:S(2)}, u32[]{:S(2)}) %collective-permute-start.14) | collective-permute-done | bytes 65568 | tf_op jit(solution)/shard_map/ppermute | solution.py:22
  75.5 0.5 convolution_convert_fusion
  76.0 1.0 copy-done.3
  77.0 1.4 %fusion.42 = (bf16[127,32,64]{0,2,1:T(8,128)(2,1)}, bf16[127,32,64]{0,2,1:T(8,128)(2,1)}) fusion(bf16[256,32,64]{0,2,1:T(8,128)(2,1)S(1)} %convolution_convert_fusion), kind=kLoop, calls=%fused_computation.76 | loop fusion | bytes 2080768 | tf_op jit(solution)/shard_map/while/body/eval_jaxpr/slice | solution.py:89
  78.4 3.5 %copy.30 = bf16[127,32,64]{2,1,0:T(8,128)(2,1)} copy(bf16[127,32,64]{0,2,1:T(8,128)(2,1)} %get-tuple-element.30) | data formatting | bytes 1040384 | tf_op jit(solution)/shard_map/while/body/eval_jaxpr/slice | solution.py:85
  81.9 3.5 %copy.34 = bf16[127,32,64]{2,1,0:T(8,128)(2,1)} copy(bf16[127,32,64]{0,2,1:T(8,128)(2,1)} %get-tuple-element.29) | data formatting | bytes 1040384 | tf_op jit(solution)/shard_map/while/body/eval_jaxpr/slice | solution.py:89
  85.4 2.7 %fusion.45 = f32[127,32,96]{2,1,0:T(8,128)S(1)} fusion(bf16[127,32,64]{2,1,0:T(8,128)(2,1)} %copy.30, bf16[127,96,64]{1,2,0:T(8,128)(2,1)} %copy.33), kind=kOutput, calls=%fused_computation.79 | convolution fusion | flops 49938432 | bytes 3641344 | tf_op jit(solution)/shard_map/while/body/eval_jaxpr/kpr,ktr->ktp/dot_general | solution.py:75
  88.2 2.0 %fusion.44 = f32[127,32,96]{2,1,0:T(8,128)} fusion(bf16[127,32,64]{2,1,0:T(8,128)(2,1)S(1)} %copy-done.4, bf16[127,96,64]{1,2,0:T(8,128)(2,1)S(1)} %copy-done.1), kind=kOutput, calls=%fused_computation.78 | convolution fusion | flops 49938432 | bytes 3641344 | tf_op jit(solution)/shard_map/while/body/eval_jaxpr/kpr,ktr->ktp/dot_general | solution.py:75
  90.2 1.6 %subtract_convert_fusion = bf16[127,32,96]{2,1,0:T(8,128)(2,1)} fusion(f32[127,32,96]{2,1,0:T(8,128)S(1)} %fusion.45, bf16[127,32,64]{2,1,0:T(8,128)(2,1)S(1)} %copy-done.5, bf16[127,96,64]{1,2,0:T(8,128)(2,1)S(1)} %copy-done.1), kind=kOutput, calls=%fused_computation.5 | convolution fusion | flops 50718720 | bytes 4421632 | tf_op jit(solution)/shard_map/while/body/eval_jaxpr/kpr,ktr->ktp/dot_general | solution.py:75
  91.8 2.7 %copy.36 = bf16[127,32,96]{0,2,1:T(8,128)(2,1)} copy(bf16[127,32,96]{2,1,0:T(8,128)(2,1)} %subtract_convert_fusion) | data formatting | bytes 1560576 | tf_op jit(solution)/shard_map/convert.4
  94.6 2.4 %copy.37 = bf16[127,3072]{1,0:T(8,128)(2,1)} copy(bf16[127,3072]{0,1:T(8,128)(2,1)} %bitcast.21) | data formatting | bytes 1560576 | tf_op jit(solution)/shard_map/while/body/eval_jaxpr/concatenate | solution.py:93
  96.9 2.9 %copy.28 = bf16[129,32,64]{2,1,0:T(8,128)(2,1)} copy(bf16[129,32,64]{0,2,1:T(8,128)(2,1)} %bitcast.20) | data formatting | bytes 1056768 | tf_op jit(solution)/shard_map/while/body/eval_jaxpr/slice | solution.py:84
  99.8 4.3 %fusion.4 = bf16[129,32,96]{2,1,0:T(8,128)(2,1)} fusion(f32[1,32,96]{2,1,0:T(8,128)S(1)} %broadcast.78, f32[127,32,96]{2,1,0:T(8,128)} %fusion.44, bf16[129,32,64]{2,1,0:T(8,128)(2,1)} %copy.28, bf16[129,96,64]{1,2,0:T(8,128)(2,1)} %copy.29), kind=kOutput, calls=%fused_computation.4 | convolution fusion | flops 52310016 | bytes 4478976 | tf_op jit(solution)/shard_map/while/body/eval_jaxpr/kpr,ktr->ktp/dot_general | solution.py:75
  104.0 3.4 %concatenate.33 = bf16[129,3072]{1,0:T(8,128)(2,1)} reshape(bf16[129,32,96]{2,1,0:T(8,128)(2,1)} %fusion.4) | data formatting | bytes 1585152 | tf_op jit(solution)/shard_map/while/body/eval_jaxpr/concatenate | solution.py:93
  107.4 2.5 %fusion.13 = f32[3072]{0:T(1024)S(1)} fusion(bf16[1,3072]{1,0:T(2,128)(2,1)S(1)} %concatenate.34, bf16[127,3072]{1,0:T(8,128)(2,1)} %copy.37, bf16[129,3072]{1,0:T(8,128)(2,1)} %concatenate.33, f32[129,256]{1,0:T(8,128)S(1)} %sine_multiply_fusion, f32[129,256]{1,0:T(8,128)S(1)} %copy-done.6), kind=kOutput, calls=%fused_computation.15 | convolution fusion | flops 413121024 | bytes 1855488 | tf_op jit(solution)/shard_map/while/body/eval_jaxpr/dot_general | solution.py:95
  110.0 0.1 select_reduce_fusion
  110.2 1.3 %collective-permute-start.16 = (f32[1,16]{0,1:T(8,128)S(1)}, f32[1,16]{0,1:T(8,128)S(1)}, u32[]{:S(2)}, u32[]{:S(2)}) collective-permute-start(f32[1,16]{0,1:T(8,128)S(1)} %get-tuple-element.36), channel_id=1, source_target_pairs={{1,0},{2,1},{3,2},{4,3},{5,4},{6,5},{7,6},{8,7},{9,8},{10,9},{11,1... | collective-permute-start | bytes 200 | tf_op jit(solution)/shard_map/ppermute | solution.py:42
  111.5 3.0 %collective-permute-start.15 = (f32[1,16]{0,1:T(8,128)S(1)}, f32[1,16]{0,1:T(8,128)S(1)}, u32[]{:S(2)}, u32[]{:S(2)}) collective-permute-start(f32[1,16]{0,1:T(8,128)S(1)} %get-tuple-element.31), channel_id=1, source_target_pairs={{0,1},{1,2},{2,3},{3,4},{4,5},{5,6},{6,7},{7,8},{8,9},{9,10},{10,1... | collective-permute-start | bytes 200 | tf_op jit(solution)/shard_map/ppermute | solution.py:41
  114.5 0.8 collective-permute-done.15
  115.3 0.7 fusion.33
  (53 shorter events, 0.7 us)
Async XLA Ops:
  0.6 8.0 %copy-start = (bf16[96,64,256]{2,1,0:T(8,128)(2,1)S(1)}, bf16[96,64,256]{2,1,0:T(8,128)(2,1)}, u32[]{:S(2)}) copy-start(bf16[96,64,256]{2,1,0:T(8,128)(2,1)} %param.5) | copy-start | bytes 9437188
  0.6 29.9 %collective-permute-start = (bf16[2,64,256]{2,1,0:T(8,128)(2,1)}, bf16[2,64,256]{2,1,0:T(8,128)(2,1)}, u32[]{:S(2)}, u32[]{:S(2)}) collective-permute-start(bf16[2,64,256]{2,1,0:T(8,128)(2,1)} %param.6), channel_id=1, source_target_pairs={{0,1},{1,2},{2,3},{3,4},{4,5},{5,6},{6,7},{7,8},{8,9},{9,10},{10,1... | collective-permute-start | bytes 196616 | tf_op jit(solution)/shard_map/ppermute | solution.py:22
  1.1 29.4 %collective-permute-start.1 = (bf16[2,64,256]{2,1,0:T(8,128)(2,1)}, bf16[2,64,256]{2,1,0:T(8,128)(2,1)}, u32[]{:S(2)}, u32[]{:S(2)}) collective-permute-start(bf16[2,64,256]{2,1,0:T(8,128)(2,1)} %param.6), channel_id=1, source_target_pairs={{0,15},{1,0},{2,1},{3,2},{4,3},{5,4},{6,5},{7,6},{8,7},{9,8},{10,9... | collective-permute-start | bytes 196616 | tf_op jit(solution)/shard_map/ppermute | solution.py:27
  12.2 2.7 %copy-start.2 = (bf16[256,96,64]{0,1,2:T(8,128)(2,1)}, bf16[256,96,64]{0,1,2:T(8,128)(2,1)S(1)}, u32[]{:S(2)}) copy-start(bf16[256,96,64]{0,1,2:T(8,128)(2,1)S(1)} %multiply_convert_fusion) | copy-start | bytes 9437188
  23.0 7.5 %copy-start.7 = (bf16[2,64,256]{2,1,0:T(8,128)(2,1)S(1)}, bf16[2,64,256]{2,1,0:T(8,128)(2,1)}, u32[]{:S(2)}) copy-start(bf16[2,64,256]{2,1,0:T(8,128)(2,1)} %param.6) | copy-start | bytes 196612
  30.5 6.7 %collective-permute-start.2 = (bf16[2,64,256]{2,1,0:T(8,128)(2,1)}, bf16[2,64,256]{2,1,0:T(8,128)(2,1)S(1)}, u32[]{:S(2)}, u32[]{:S(2)}) collective-permute-start(bf16[2,64,256]{2,1,0:T(8,128)(2,1)} %collective-permute-done), channel_id=1, source_target_pairs={{0,1},{1,2},{2,3},{3,4},{4,5},{5,6},{6,7},{7,8},{8,9},{9,10},{10,1... | collective-permute-start | bytes 196616 | tf_op jit(solution)/shard_map/ppermute | solution.py:22
  30.6 6.6 %collective-permute-start.3 = (bf16[2,64,256]{2,1,0:T(8,128)(2,1)}, bf16[2,64,256]{2,1,0:T(8,128)(2,1)S(1)}, u32[]{:S(2)}, u32[]{:S(2)}) collective-permute-start(bf16[2,64,256]{2,1,0:T(8,128)(2,1)} %collective-permute-done.1), channel_id=1, source_target_pairs={{0,15},{1,0},{2,1},{3,2},{4,3},{5,4},{6,5},{7,6},{8,7},{9,8},{10,9... | collective-permute-start | bytes 196616 | tf_op jit(solution)/shard_map/ppermute | solution.py:27
  37.2 6.4 %collective-permute-start.4 = (bf16[2,64,256]{2,1,0:T(8,128)(2,1)S(1)}, bf16[2,64,256]{2,1,0:T(8,128)(2,1)S(1)}, u32[]{:S(2)}, u32[]{:S(2)}) collective-permute-start(bf16[2,64,256]{2,1,0:T(8,128)(2,1)S(1)} %collective-permute-done.2), channel_id=1, source_target_pairs={{0,1},{1,2},{2,3},{3,4},{4,5},{5,6},{6,7},{7,8},{8,9},{9,10},{10,1... | collective-permute-start | bytes 196616 | tf_op jit(solution)/shard_map/ppermute | solution.py:22
  37.2 6.3 %collective-permute-start.5 = (bf16[2,64,256]{2,1,0:T(8,128)(2,1)S(1)}, bf16[2,64,256]{2,1,0:T(8,128)(2,1)S(1)}, u32[]{:S(2)}, u32[]{:S(2)}) collective-permute-start(bf16[2,64,256]{2,1,0:T(8,128)(2,1)S(1)} %collective-permute-done.3), channel_id=1, source_target_pairs={{0,15},{1,0},{2,1},{3,2},{4,3},{5,4},{6,5},{7,6},{8,7},{9,8},{10,9... | collective-permute-start | bytes 196616 | tf_op jit(solution)/shard_map/ppermute | solution.py:27
  43.6 6.4 %collective-permute-start.6 = (bf16[2,64,256]{2,1,0:T(8,128)(2,1)S(1)}, bf16[2,64,256]{2,1,0:T(8,128)(2,1)S(1)}, u32[]{:S(2)}, u32[]{:S(2)}) collective-permute-start(bf16[2,64,256]{2,1,0:T(8,128)(2,1)S(1)} %collective-permute-done.4), channel_id=1, source_target_pairs={{0,1},{1,2},{2,3},{3,4},{4,5},{5,6},{6,7},{7,8},{8,9},{9,10},{10,1... | collective-permute-start | bytes 196616 | tf_op jit(solution)/shard_map/ppermute | solution.py:22
  43.6 6.4 %collective-permute-start.7 = (bf16[2,64,256]{2,1,0:T(8,128)(2,1)S(1)}, bf16[2,64,256]{2,1,0:T(8,128)(2,1)S(1)}, u32[]{:S(2)}, u32[]{:S(2)}) collective-permute-start(bf16[2,64,256]{2,1,0:T(8,128)(2,1)S(1)} %collective-permute-done.5), channel_id=1, source_target_pairs={{0,15},{1,0},{2,1},{3,2},{4,3},{5,4},{6,5},{7,6},{8,7},{9,8},{10,9... | collective-permute-start | bytes 196616 | tf_op jit(solution)/shard_map/ppermute | solution.py:27
  50.0 6.4 %collective-permute-start.8 = (bf16[2,64,256]{2,1,0:T(8,128)(2,1)S(1)}, bf16[2,64,256]{2,1,0:T(8,128)(2,1)S(1)}, u32[]{:S(2)}, u32[]{:S(2)}) collective-permute-start(bf16[2,64,256]{2,1,0:T(8,128)(2,1)S(1)} %collective-permute-done.6), channel_id=1, source_target_pairs={{0,1},{1,2},{2,3},{3,4},{4,5},{5,6},{6,7},{7,8},{8,9},{9,10},{10,1... | collective-permute-start | bytes 196616 | tf_op jit(solution)/shard_map/ppermute | solution.py:22
  50.0 6.4 %collective-permute-start.9 = (bf16[2,64,256]{2,1,0:T(8,128)(2,1)S(1)}, bf16[2,64,256]{2,1,0:T(8,128)(2,1)S(1)}, u32[]{:S(2)}, u32[]{:S(2)}) collective-permute-start(bf16[2,64,256]{2,1,0:T(8,128)(2,1)S(1)} %collective-permute-done.7), channel_id=1, source_target_pairs={{0,15},{1,0},{2,1},{3,2},{4,3},{5,4},{6,5},{7,6},{8,7},{9,8},{10,9... | collective-permute-start | bytes 196616 | tf_op jit(solution)/shard_map/ppermute | solution.py:27
  56.3 6.4 %collective-permute-start.10 = (bf16[2,64,256]{2,1,0:T(8,128)(2,1)S(1)}, bf16[2,64,256]{2,1,0:T(8,128)(2,1)S(1)}, u32[]{:S(2)}, u32[]{:S(2)}) collective-permute-start(bf16[2,64,256]{2,1,0:T(8,128)(2,1)S(1)} %collective-permute-done.8), channel_id=1, source_target_pairs={{0,1},{1,2},{2,3},{3,4},{4,5},{5,6},{6,7},{7,8},{8,9},{9,10},{10,1... | collective-permute-start | bytes 196616 | tf_op jit(solution)/shard_map/ppermute | solution.py:22
  56.4 6.4 %collective-permute-start.11 = (bf16[2,64,256]{2,1,0:T(8,128)(2,1)S(1)}, bf16[2,64,256]{2,1,0:T(8,128)(2,1)S(1)}, u32[]{:S(2)}, u32[]{:S(2)}) collective-permute-start(bf16[2,64,256]{2,1,0:T(8,128)(2,1)S(1)} %collective-permute-done.9), channel_id=1, source_target_pairs={{0,15},{1,0},{2,1},{3,2},{4,3},{5,4},{6,5},{7,6},{8,7},{9,8},{10,9... | collective-permute-start | bytes 196616 | tf_op jit(solution)/shard_map/ppermute | solution.py:27
  62.7 6.4 %collective-permute-start.12 = (bf16[2,64,256]{2,1,0:T(8,128)(2,1)S(1)}, bf16[2,64,256]{2,1,0:T(8,128)(2,1)S(1)}, u32[]{:S(2)}, u32[]{:S(2)}) collective-permute-start(bf16[2,64,256]{2,1,0:T(8,128)(2,1)S(1)} %collective-permute-done.10), channel_id=1, source_target_pairs={{0,1},{1,2},{2,3},{3,4},{4,5},{5,6},{6,7},{7,8},{8,9},{9,10},{10,1... | collective-permute-start | bytes 196616 | tf_op jit(solution)/shard_map/ppermute | solution.py:22
  62.8 6.4 %collective-permute-start.13 = (bf16[2,64,256]{2,1,0:T(8,128)(2,1)S(1)}, bf16[2,64,256]{2,1,0:T(8,128)(2,1)S(1)}, u32[]{:S(2)}, u32[]{:S(2)}) collective-permute-start(bf16[2,64,256]{2,1,0:T(8,128)(2,1)S(1)} %collective-permute-done.11), channel_id=1, source_target_pairs={{0,15},{1,0},{2,1},{3,2},{4,3},{5,4},{6,5},{7,6},{8,7},{9,8},{10,9... | collective-permute-start | bytes 196616 | tf_op jit(solution)/shard_map/ppermute | solution.py:27
  69.1 6.4 %collective-permute-start.14 = (bf16[2,64,256]{2,1,0:T(8,128)(2,1)S(1)}, bf16[2,64,256]{2,1,0:T(8,128)(2,1)S(1)}, u32[]{:S(2)}, u32[]{:S(2)}) collective-permute-start(bf16[2,64,256]{2,1,0:T(8,128)(2,1)S(1)} %collective-permute-done.12), channel_id=1, source_target_pairs={{0,1},{1,2},{2,3},{3,4},{4,5},{5,6},{6,7},{7,8},{8,9},{9,10},{10,1... | collective-permute-start | bytes 196616 | tf_op jit(solution)/shard_map/ppermute | solution.py:22
  76.0 1.0 copy-start.3
  85.4 2.7 %copy-start.1 = (bf16[127,96,64]{1,2,0:T(8,128)(2,1)S(1)}, bf16[127,96,64]{1,2,0:T(8,128)(2,1)}, u32[]{:S(2)}) copy-start(bf16[127,96,64]{1,2,0:T(8,128)(2,1)} %copy.31) | copy-start | bytes 4681732
  85.4 2.8 %copy-start.4 = (bf16[127,32,64]{2,1,0:T(8,128)(2,1)S(1)}, bf16[127,32,64]{2,1,0:T(8,128)(2,1)}, u32[]{:S(2)}) copy-start(bf16[127,32,64]{2,1,0:T(8,128)(2,1)} %copy.30) | copy-start | bytes 1560580
  88.2 2.0 %copy-start.5 = (bf16[127,32,64]{2,1,0:T(8,128)(2,1)S(1)}, bf16[127,32,64]{2,1,0:T(8,128)(2,1)}, u32[]{:S(2)}) copy-start(bf16[127,32,64]{2,1,0:T(8,128)(2,1)} %copy.34) | copy-start | bytes 1560580
  99.8 7.6 %copy-start.6 = (f32[129,256]{1,0:T(8,128)S(1)}, f32[129,256]{1,0:T(8,128)}, u32[]{:S(2)}) copy-start(f32[129,256]{1,0:T(8,128)} %cosine_multiply_fusion) | copy-start | bytes 396292
  109.9 6.1 %copy-start.8 = (f32[32,96]{1,0:T(8,128)}, f32[32,96]{1,0:T(8,128)S(1)}, u32[]{:S(2)}) copy-start(f32[32,96]{1,0:T(8,128)S(1)} %reshape.51) | copy-start | bytes 36868
  110.2 4.3 %collective-permute-start.16 = (f32[1,16]{0,1:T(8,128)S(1)}, f32[1,16]{0,1:T(8,128)S(1)}, u32[]{:S(2)}, u32[]{:S(2)}) collective-permute-start(f32[1,16]{0,1:T(8,128)S(1)} %get-tuple-element.36), channel_id=1, source_target_pairs={{1,0},{2,1},{3,2},{4,3},{5,4},{6,5},{7,6},{8,7},{9,8},{10,9},{11,1... | collective-permute-start | bytes 200 | tf_op jit(solution)/shard_map/ppermute | solution.py:42
  111.5 3.8 %collective-permute-start.15 = (f32[1,16]{0,1:T(8,128)S(1)}, f32[1,16]{0,1:T(8,128)S(1)}, u32[]{:S(2)}, u32[]{:S(2)}) collective-permute-start(f32[1,16]{0,1:T(8,128)S(1)} %get-tuple-element.31), channel_id=1, source_target_pairs={{0,1},{1,2},{2,3},{3,4},{4,5},{5,6},{6,7},{7,8},{8,9},{9,10},{10,1... | collective-permute-start | bytes 200 | tf_op jit(solution)/shard_map/ppermute | solution.py:41
